TPU v7x, 32 devices: a whole 2x2x4 slice. The times are simulated.
32 devices in a mesh: pool: 8 (over z, core), band: 4 (over y, x).
Axes of the slice: x: 2, y: 2, z: 4, core: 2. Of those that a mesh axis runs over, the one named last changes fastest.
Arguments:
- orbitals: float32 [8, 4, 2, 13824], P('pool', 'band'), may hold values from -6 to 6
- kpoints: float32 [8, 3], replicated, may hold values from -0.5 to 0.5
- owner: int32 [1], replicated, may hold values from 0 to 7
Outputs:
- exchange: float32 [8, 4, 2, 13824], P('pool', 'band')
All inputs are finite; a program needn't handle non-finite values.
Results may differ from a plain program's by a relative error of at most 0.0001.
Values sent between devices are 32-bit elements; how exact they have to be, the bound alone decides.
A program may use at most 64 MiB of HBM per device.

v0:
```python
import math

import jax
import jax.numpy as jnp
from jax import lax
from jax.sharding import PartitionSpec as P

NG = 24


mixing = 0.25
kernel_scale = 60.0
screening = 4.0


def frequencies():
    idx = jnp.arange(NG, dtype=jnp.int32)
    return ((idx + NG // 2) % NG - NG // 2).astype(jnp.float32)


def coulomb(dvec):
    freq = frequencies()
    square = (
        (freq[:, None, None] + dvec[0]) ** 2
        + (freq[None, :, None] + dvec[1]) ** 2
        + (freq[None, None, :] + dvec[2]) ** 2
    )
    return (kernel_scale / (square + screening)).reshape(-1)


def dft_matrix(direction, factor):
    idx = jnp.arange(NG, dtype=jnp.int32)
    phase = (idx[:, None] * idx[None, :] % NG).astype(jnp.float32) * (2.0 * math.pi / NG)
    cosine = jnp.cos(phase) * factor
    sine = direction * jnp.sin(phase) * factor
    upper = jnp.concatenate([cosine, -sine], axis=1)
    lower = jnp.concatenate([sine, cosine], axis=1)
    return jnp.concatenate([upper, lower], axis=0)


def transform(field, matrix):
    batch = field.shape[0]
    work = field.reshape(batch, 2 * NG, NG * NG)
    for turn in range(3):
        work = jnp.einsum("ij,pjk->pik", matrix, work, precision=lax.Precision.HIGHEST)
        work = (
            work.reshape(batch, 2, NG, NG, NG)
            .transpose(0, 1, 3, 4, 2)
            .reshape(batch, 2 * NG, NG * NG)
        )
    return work.reshape(batch, 2, NG * NG * NG)


def contribution(sources, resident, kernel, forward, inverse):
    count_s = sources.shape[0]
    count_r = resident.shape[0]
    src_re = sources[:, 0][:, None, :]
    src_im = sources[:, 1][:, None, :]
    res_re = resident[:, 0][None, :, :]
    res_im = resident[:, 1][None, :, :]
    dens_re = src_re * res_re + src_im * res_im
    dens_im = src_re * res_im - src_im * res_re
    density = jnp.stack([dens_re, dens_im], axis=2).reshape(count_s * count_r, 2, -1)
    spectrum = transform(density, forward) * kernel
    potential = transform(spectrum, inverse).reshape(count_s, count_r, 2, -1)
    pot_re = potential[:, :, 0]
    pot_im = potential[:, :, 1]
    out_re = -mixing * jnp.sum(src_re * pot_re - src_im * pot_im, axis=0)
    out_im = -mixing * jnp.sum(src_re * pot_im + src_im * pot_re, axis=0)
    return jnp.stack([out_re, out_im], axis=1)


def shards(orbitals, kpoints, owner):
    resident = orbitals[0]
    pool_index = lax.axis_index("pool")
    kvec = lax.dynamic_index_in_dim(kpoints, pool_index, 0, keepdims=False)
    forward = dft_matrix(-1.0, 1.0)
    inverse = dft_matrix(1.0, 1.0 / NG)
    source_k = owner[0]
    qvec = lax.dynamic_index_in_dim(kpoints, source_k, 0, keepdims=False)
    kernel = coulomb(kvec - qvec)
    masked = jnp.where(pool_index == source_k, resident, jnp.zeros_like(resident))
    sources = lax.psum(masked, "pool")
    total = contribution(
        lax.all_gather(sources, "band", axis=0, tiled=True), resident, kernel, forward, inverse
    )
    return total[None]


def solution(mesh):
    placed = (P("pool", "band", None, None), P(), P())
    return jax.shard_map(
        shards, mesh=mesh, in_specs=placed, out_specs=P("pool", "band", None, None), check_vma=False
    )
```

profile of v0, /device:TPU:0, one launch (start us, length us, event | category | flops | bytes accessed | tf_op | source)
XLA Modules:
  0.0 121.5 jit_solution(5851988328339792703)
XLA Ops:
  6.5 0.0 all-reduce.2.cloned.1.call-start
  7.2 1.6 %broadcast_select_fusion = f32[1,2,13824]{2,1,0:T(2,128)} fusion(pred[]{:T(512)S(6)} %eq.8, f32[1,1,2,13824]{3,2,1,0:T(2,128)} %param.3), kind=kLoop, calls=%fused_computation.16 | loop fusion | flops 27648 | bytes 221185 | tf_op jit(solution)/shard_map/jit(_where)/select_n | solution.py:82
  8.8 0.0 all-reduce.2.cloned.1.call-update
  8.8 0.1 fusion.7
  8.9 0.1 fusion.11
  9.0 0.1 fusion.8
  9.0 1.3 %slice_reduce_fusion.1 = (f32[13824]{0:T(1024)S(1)}, f32[13824]{0:T(1024)S(1)}) fusion(f32[1,2,13824]{2,1,0:T(2,128)} %bitcast.81), kind=kLoop, calls=%fused_computation.19 | loop fusion | bytes 221184 | tf_op jit(solution)/shard_map/slice | solution.py:59
  10.3 0.8 dynamic-slice_subtract_fusion
  11.2 0.6 fusion.21
  11.8 0.7 add_multiply_fusion.2
  12.5 1.3 %add_multiply_fusion = (f32[24]{0:T(128)S(1)}, f32[24]{0:T(128)S(1)}) fusion(f32[]{:T(128)} %bitcast.13, f32[]{:T(128)} %bitcast.12), kind=kLoop, calls=%fused_computation.43 | loop fusion | flops 312 | bytes 200 | tf_op jit(solution)/shard_map/integer_pow | solution.py:26
  13.7 0.1 broadcast_add_fusion
  13.8 0.1 add.188
  13.9 0.1 add.189
  14.1 0.1 add.193
  14.2 0.1 fusion.12
  14.3 50.5 %all-reduce.2.cloned.1.call-done = f32[1,2,13824]{2,1,0:T(2,128)} async-done(((f32[1,2,13824]{2,1,0:T(2,128)}), f32[1,2,13824]{2,1,0:T(2,128)}) %all-reduce.2.cloned.1.call-update) | async-done | bytes 110608 | tf_op jit(solution)/shard_map/psum | solution.py:83
  64.8 10.0 %all_gather.3 = f32[4,2,13824]{2,1,0:T(2,128)S(1)} all-gather(f32[1,2,13824]{2,1,0:T(2,128)} %all-reduce.2.cloned.1.call-done), channel_id=1, replica_groups=mesh['pool'=8,'band'=4] {'band'}, dimensions={0}, use_global_device_ids=true | all-gather | bytes 552960 | tf_op jit(solution)/shard_map/all_gather | solution.py:85
  74.8 0.5 add_bitcast_fusion
  75.3 1.4 %maximum_reduce_fusion = f32[4,2,13824]{2,1,0:T(2,128)S(1)} fusion(f32[4,1,1,13824]{3,1,2,0:T(1,128)S(1)} %get-tuple-element.10, f32[4,1,1,13824]{3,1,2,0:T(1,128)S(1)} %get-tuple-element.9), kind=kLoop, calls=%fused_computation.7 | loop fusion | flops 110592 | bytes 884736 | tf_op jit(solution)/shard_map/stack | solution.py:63
  76.7 0.4 reshape_reshape.6
  77.1 0.6 convolution_bitcast_fusion.5
  77.7 0.9 reshape.181
  78.6 2.2 %copy.10 = f32[4,2,24,24,24]{4,3,2,1,0:T(8,128)} copy(f32[4,2,24,24,24]{3,2,4,1,0:T(8,128)S(1)} %bitcast.74) | data formatting | bytes 884736 | tf_op jit(solution)/shard_map/transpose | solution.py:48
  80.8 2.2 %reshape.182 = f32[4,48,576]{2,1,0:T(8,128)S(1)} reshape(f32[4,2,24,24,24]{4,3,2,1,0:T(8,128)} %copy.10) | data formatting | bytes 884736 | tf_op jit(solution)/shard_map/reshape | solution.py:49
  83.0 0.6 convolution_bitcast_fusion.4
  83.6 0.9 reshape.183
  84.5 2.0 %copy.11 = f32[4,2,24,24,24]{4,3,2,1,0:T(8,128)} copy(f32[4,2,24,24,24]{3,2,4,1,0:T(8,128)S(1)} %bitcast.75) | data formatting | bytes 884736 | tf_op jit(solution)/shard_map/transpose | solution.py:48
  86.5 2.2 %reshape.184 = f32[4,48,576]{2,1,0:T(8,128)S(1)} reshape(f32[4,2,24,24,24]{4,3,2,1,0:T(8,128)} %copy.11) | data formatting | bytes 884736 | tf_op jit(solution)/shard_map/reshape | solution.py:49
  88.7 0.6 convolution_bitcast_fusion.3
  89.3 0.9 reshape.185
  90.2 2.0 %copy.12 = f32[4,2,24,24,24]{4,3,2,1,0:T(8,128)} copy(f32[4,2,24,24,24]{3,2,4,1,0:T(8,128)S(1)} %bitcast.76) | data formatting | bytes 884736 | tf_op jit(solution)/shard_map/transpose | solution.py:48
  92.2 2.2 %reshape_reshape.7 = f32[4,48,576]{2,1,0:T(8,128)S(1)} reshape(f32[4,2,24,24,24]{4,3,2,1,0:T(8,128)} %copy.12) | data formatting | bytes 884736 | tf_op jit(solution)/shard_map/reshape;reshape | solution.py:51
  94.5 0.6 convolution_bitcast_fusion.2
  95.1 0.9 reshape.186
  96.0 2.0 %copy.13 = f32[4,2,24,24,24]{4,3,2,1,0:T(8,128)} copy(f32[4,2,24,24,24]{3,2,4,1,0:T(8,128)S(1)} %bitcast.77) | data formatting | bytes 884736 | tf_op jit(solution)/shard_map/transpose | solution.py:48
  97.9 2.2 %reshape.187 = f32[4,48,576]{2,1,0:T(8,128)S(1)} reshape(f32[4,2,24,24,24]{4,3,2,1,0:T(8,128)} %copy.13) | data formatting | bytes 884736 | tf_op jit(solution)/shard_map/reshape | solution.py:49
  100.2 0.6 convolution_bitcast_fusion.1
  100.8 0.9 reshape.188
  101.7 2.0 %copy.14 = f32[4,2,24,24,24]{4,3,2,1,0:T(8,128)} copy(f32[4,2,24,24,24]{3,2,4,1,0:T(8,128)S(1)} %bitcast.78) | data formatting | bytes 884736 | tf_op jit(solution)/shard_map/transpose | solution.py:48
  103.7 2.5 %reshape.189 = f32[4,48,576]{2,1,0:T(8,128)S(1)} reshape(f32[4,2,24,24,24]{4,3,2,1,0:T(8,128)} %copy.14) | data formatting | bytes 884736 | tf_op jit(solution)/shard_map/reshape | solution.py:49
  106.1 0.6 convolution_bitcast_fusion
  106.7 0.9 reshape.190
  107.6 2.0 %copy.15 = f32[4,2,24,24,24]{4,3,2,1,0:T(8,128)} copy(f32[4,2,24,24,24]{3,2,4,1,0:T(8,128)S(1)} %bitcast.79) | data formatting | bytes 884736 | tf_op jit(solution)/shard_map/transpose | solution.py:48
  109.6 3.3 %reshape_reshape_reshape.3 = f32[4,1,2,13824]{3,1,2,0:T(1,128)S(1)} reshape(f32[4,2,24,24,24]{4,3,2,1,0:T(8,128)} %copy.15) | data formatting | bytes 884736 | tf_op jit(solution)/shard_map/reshape;reshape;reshape | solution.py:65
  112.9 0.9 subtract_reduce_fusion
  113.9 0.7 maximum_bitcast_fusion
  (7 shorter events, 0.1 us)
Async XLA Ops:
  6.5 58.3 %all-reduce.2.cloned.1.call-start = ((), (), s32[]{:S(2)}) async-start(), calls=%async_computation | async-start | bytes 221184 | tf_op jit(solution)/shard_map/psum | solution.py:83
Sparse Core Ops, SparseCore 0:
  9.7 55.0 all-reduce.1
where the time goes:
time: 123 us; the launch traced here: 122 us
  waiting for transfers between devices  50.5 us (41%)
  local copies, waits for them, and re-layouts  34.8 us (28%)
  between operations  14.3 us (12%)
  blocking collectives  10 us (8%)
  other arithmetic  8.27 us (7%)
  matrix products  3.56 us (3%)
    psum x1, waiting for transfers between devices, shards(): sources = lax.psum(masked, 'pool')  50.5 us
    transpose x6, local copies, waits for them, and re-layouts, transform(): work = work.reshape(batch, 2, NG, NG, NG).transpose(0, 1, 3, 4, 2).reshap...  12 us
    all_gather x1, blocking collectives, shards(): lax.all_gather(sources, 'band', axis=0, tiled=True)  10 us
    reshape x4, local copies, waits for them, and re-layouts, transform(): work = work.reshape(batch, 2, NG, NG, NG).transpose(0, 1, 3, 4, 2).reshap...  9.21 us
    reshape x6, local copies, waits for them, and re-layouts, transform(): work.reshape(batch, 2, NG, NG, NG).transpose(0, 1, 3, 4, 2)  5.29 us
    dot_general x6, matrix products, transform(): jnp.einsum('ij,pjk->pik', matrix, work, precision=lax.Precision.HIGHEST)  3.56 us
    another operation x1, local copies, waits for them, and re-layouts, contribution(): potential = transform(spectrum, inverse).reshape(count_s, count_r, 2, -1)  3.31 us
  transfers between devices with their start and end apart: 1, of which 1 were waited for; matrix products, arithmetic and copies ran while one was open for 4% of the time, Pallas kernels for 0%

commit v1 on v0

v1 whole, which is shorter than its diff:
```python
import functools
import math

import jax
import jax.numpy as jnp
import numpy as np
from jax import lax
from jax.experimental import pallas as pl
from jax.experimental.pallas import tpu as pltpu
from jax.sharding import PartitionSpec as P

NG = 24
ROWS = NG * NG
GRID = NG**3
LANES = 128
TILES = GRID // LANES
GROUP = 4

mixing = 0.25
kernel_scale = 60.0
screening = 4.0

MESH = pl.DeviceIdType.MESH


def dft_weights():
    idx = np.arange(NG)
    phase = 2.0 * np.pi * (np.outer(idx, idx) % NG) / NG
    cosine, sine = np.cos(phase), -np.sin(phase)
    full = np.zeros((2 * LANES, 2 * LANES))
    for n in range(GROUP):
        lo = n * NG
        re, im = slice(lo, lo + NG), slice(LANES + lo, LANES + lo + NG)
        full[re, re] = cosine
        full[re, im] = sine
        full[im, re] = -sine
        full[im, im] = cosine
    full = full.astype(np.float32)
    high = full.astype(jnp.bfloat16)
    low = (full - high.astype(np.float32)).astype(jnp.bfloat16)
    return np.stack([high, low])


def cadd(x, y):
    return x[0] + y[0], x[1] + y[1]


def csub(x, y):
    return x[0] - y[0], x[1] - y[1]


def down(x):
    return x[1], -x[0]


def dft3(x0, x1, x2):
    total = cadd(x1, x2)
    diff = csub(x1, x2)
    half = (x0[0] - 0.5 * total[0], x0[1] - 0.5 * total[1])
    root = math.sqrt(3.0) / 2.0
    turn = (root * diff[1], -root * diff[0])
    return cadd(x0, total), cadd(half, turn), csub(half, turn)


def dft4(x0, x1, x2, x3):
    a, b = cadd(x0, x2), csub(x0, x2)
    c, d = cadd(x1, x3), down(csub(x1, x3))
    return cadd(a, c), cadd(b, d), csub(a, c), csub(b, d)


def dft8(x):
    even = dft4(x[0], x[2], x[4], x[6])
    odd = dft4(x[1], x[3], x[5], x[7])
    root = math.sqrt(0.5)
    one, three = odd[1], odd[3]
    twisted = [
        odd[0],
        (root * (one[0] + one[1]), root * (one[1] - one[0])),
        down(odd[2]),
        (root * (three[1] - three[0]), -root * (three[0] + three[1])),
    ]
    return [cadd(even[i], twisted[i]) for i in range(4)] + [csub(even[i], twisted[i]) for i in range(4)]


def dft24(x):
    parts = [[None] * 8 for _ in range(3)]
    for n2 in range(8):
        three = dft3(*(x[(8 * n1 + 3 * n2) % NG] for n1 in range(3)))
        for k1 in range(3):
            parts[k1][n2] = three[k1]
    out = [None] * NG
    for k1 in range(3):
        eight = dft8(parts[k1])
        for k2 in range(8):
            out[next(k for k in range(NG) if k % 3 == k1 and k % 8 == k2)] = eight[k2]
    return out


def lane_iota(shape):
    return lax.broadcasted_iota(jnp.int32, shape, len(shape) - 1)


def starts():
    return [min(8 * i, 28) for i in range(5)]


def compute_kernel(count, owner_ref, kp_ref, src_ref, own_ref, w_ref, out_ref, sre, sim, dre, dim, acc_re, acc_im, ker):
    pool = lax.axis_index("pool")
    source = owner_ref[0]
    d0 = kp_ref[pool, 0] - kp_ref[source, 0]
    d1 = kp_ref[pool, 1] - kp_ref[source, 1]
    d2 = kp_ref[pool, 2] - kp_ref[source, 2]
    lane = lane_iota((NG, LANES))
    gc = ((lane % NG + NG // 2) % NG - NG // 2).astype(jnp.float32)
    row = lax.broadcasted_iota(jnp.int32, (NG, LANES), 0)
    gb = ((row + NG // 2) % NG - NG // 2).astype(jnp.float32)
    plane = (gb + d1) ** 2 + (gc + d2) ** 2 + screening
    for a in range(NG):
        ga = float((a + NG // 2) % NG - NG // 2)
        ker[pl.ds(NG * a, NG), :] = (kernel_scale / GRID) / (plane + (ga + d0) ** 2)

    lane8 = lane_iota((8, LANES))

    def windows(ref, base, start, ri):
        return [ref[pl.ds(base + 6 * start + 2 * s + ri, 8, stride=6), :] for s in range(3)]

    def window(rows, j):
        s, off = divmod(24 * j, LANES)
        value = rows[s]
        if off + NG > LANES:
            value = jnp.where(lane8 >= off, value, rows[s + 1])
        return value, off

    def shift(value, amount):
        amount %= LANES
        return pltpu.roll(value, amount, 1) if amount else value

    def spread(sets, j):
        total = None
        for n in range(GROUP):
            value, off = window(sets[n], j)
            moved = shift(value, NG * n - off)
            total = moved if total is None else jnp.where(lane8 >= NG * n, moved, total)
        return jnp.where(lane8 < NG * GROUP, total, 0.0)

    def line(re_ref, im_ref, first, stride, step, swapped):
        values = []
        for i in range(NG):
            at = pl.ds(first + step * i, 8, stride=stride) if stride > 1 else pl.ds(first + step * i, 8)
            pair = (re_ref[at, :], im_ref[at, :])
            values.append(pair[::-1] if swapped else pair)
        for i, pair in enumerate(dft24(values)):
            at = pl.ds(first + step * i, 8, stride=stride) if stride > 1 else pl.ds(first + step * i, 8)
            if swapped:
                pair = pair[::-1]
            re_ref[at, :] = pair[0]
            im_ref[at, :] = pair[1]

    def product(first, second):
        x = jnp.concatenate([first, second], axis=1)
        high = x.astype(jnp.bfloat16)
        low = (x - high.astype(jnp.float32)).astype(jnp.bfloat16)
        dot = functools.partial(jnp.dot, preferred_element_type=jnp.float32)
        y = dot(high, w_ref[0]) + (dot(low, w_ref[0]) + dot(high, w_ref[1]))
        return y[:, :LANES], y[:, LANES:]

    for group in range(count // GROUP):
        for start in starts():
            own = [windows(own_ref, 0, start, ri) for ri in range(2)]
            src = [
                [windows(src_ref, 2 * TILES * (group * GROUP + n), start, ri) for n in range(GROUP)]
                for ri in range(2)
            ]
            for j in range(16):
                at = pl.ds(16 * start + j, 8, stride=16)
                r_re = spread([own[0]] * GROUP, j)
                r_im = spread([own[1]] * GROUP, j)
                s_re = spread(src[0], j)
                s_im = spread(src[1], j)
                sre[at, :] = s_re
                sim[at, :] = s_im
                dre[at, :] = s_re * r_re + s_im * r_im
                dim[at, :] = s_re * r_im - s_im * r_re
        for bg in range(3):
            line(dre, dim, 8 * bg, 1, NG, False)
        for ag in range(3):
            line(dre, dim, 8 * NG * ag, NG, 1, False)
        for part in range(3):
            at = pl.ds(192 * part, 192)
            re, im = product(dre[at, :], dim[at, :])
            value = ker[at, :]
            im, re = product(im * value, re * value)
            dre[at, :] = re
            dim[at, :] = im
        for ag in range(3):
            line(dre, dim, 8 * NG * ag, NG, 1, True)
        for bg in range(3):
            line(dre, dim, 8 * bg, 1, NG, True)
        for part in range(9):
            at = pl.ds(64 * part, 64)
            s_re, s_im, p_re, p_im = sre[at, :], sim[at, :], dre[at, :], dim[at, :]
            o_re = s_re * p_re - s_im * p_im
            o_im = s_re * p_im + s_im * p_re
            if group:
                o_re += acc_re[at, :]
                o_im += acc_im[at, :]
            acc_re[at, :] = o_re
            acc_im[at, :] = o_im

    for start in starts():
        for ri, acc in enumerate((acc_re, acc_im)):
            rows = [None] * 3
            for j in range(16):
                value = acc[pl.ds(16 * start + j, 8, stride=16), :]
                value = value + shift(value, -2 * NG)
                value = value + shift(value, -NG)
                s, off = divmod(24 * j, LANES)
                moved = shift(value, off)
                rows[s] = moved if rows[s] is None else jnp.where(lane8 >= off, moved, rows[s])
                if off + NG > LANES:
                    rows[s + 1] = moved
            for s in range(3):
                out_ref[pl.ds(6 * start + 2 * s + ri, 8, stride=6), :] = -mixing * rows[s]


def compute(owner, kpoints, sources, own, weights):
    count = sources.shape[0] // (2 * TILES)
    vmem = pl.BlockSpec(memory_space=pltpu.VMEM)
    smem = pl.BlockSpec(memory_space=pltpu.SMEM)
    return pl.pallas_call(
        functools.partial(compute_kernel, count),
        out_shape=jax.ShapeDtypeStruct((2 * TILES, LANES), jnp.float32),
        in_specs=[smem, smem, vmem, vmem, vmem],
        out_specs=vmem,
        scratch_shapes=[pltpu.VMEM((ROWS, LANES), jnp.float32)] * 7,
        name="exchange",
    )(owner, kpoints, sources, own, weights)


def gather_kernel(npool, nband, owner_ref, x_ref, out_ref, pair, mine, up, dn, upo, dno, chosen,
                  s_pair, r_pair, s_up, r_up, s_dn, r_dn, s_band, r_band, s_rel, r_rel):
    pool, band = lax.axis_index("pool"), lax.axis_index("band")
    nz = npool // 2
    z, core = pool // 2, pool % 2
    half = TILES // 2
    source = owner_ref[0]
    partner = {"pool": 2 * z + 1 - core}
    above = {"pool": lax.rem(pool + 2, npool)}
    below = {"pool": lax.rem(pool + npool - 2, npool)}
    barrier = pltpu.get_barrier_semaphore()
    pl.semaphore_signal(barrier, inc=1, device_id=partner, device_id_type=MESH)
    pl.semaphore_signal(barrier, inc=1, device_id=above, device_id_type=MESH)
    pl.semaphore_signal(barrier, inc=1, device_id=below, device_id_type=MESH)
    for step in range(1, nband):
        pl.semaphore_signal(barrier, inc=1, device_id={"band": lax.rem(band + step, nband)}, device_id_type=MESH)
    pl.semaphore_wait(barrier, 3 + nband - 1)

    def remote(src, dst, ss, rs, to):
        return pltpu.make_async_remote_copy(src_ref=src, dst_ref=dst, send_sem=ss, recv_sem=rs, device_id=to, device_id_type=MESH)

    swap = remote(x_ref.at[pl.ds(half * (1 - core), half)], pair, s_pair, r_pair, partner)
    swap.start()
    swap.wait_recv()
    keep = x_ref[pl.ds(half * core, half)]
    got = pair[...]
    zero = jnp.zeros_like(got)
    mine[...] = jnp.where(source == pool, keep, jnp.where(source == 2 * z + 1 - core, got, zero))

    rise = remote(upo, up, s_up, r_up, above)
    fall = remote(dno, dn, s_dn, r_dn, below)

    def go_up():
        @pl.when(z > 0)
        def _():
            rise.wait_recv()

        @pl.when(z == 0)
        def _():
            up[...] = jnp.zeros_like(up)

        @pl.when(z < nz - 1)
        def _():
            upo[...] = up[...] + mine[...]
            rise.start()

    def go_down():
        @pl.when(z < nz - 1)
        def _():
            fall.wait_recv()

        @pl.when(z == nz - 1)
        def _():
            dn[...] = jnp.zeros_like(dn)

        @pl.when(z > 0)
        def _():
            dno[...] = dn[...] + mine[...]
            fall.start()

    @pl.when(z < nz // 2)
    def _():
        go_up()
        go_down()

    @pl.when(z >= nz // 2)
    def _():
        go_down()
        go_up()

    chosen[...] = mine[...] + up[...] + dn[...]
    mine_half = pl.ds(half * core, half)
    here = out_ref.at[band, mine_half]
    sends = []
    for step in range(1, nband):
        other = lax.rem(band + step, nband)
        copy = remote(chosen, here, s_band.at[step], r_band.at[step], {"band": other})
        copy.start()
        sends.append(copy)
    relays = [remote(chosen, here, s_rel.at[0], r_rel.at[0], partner)]
    relays[0].start()
    out_ref[band, mine_half] = chosen[...]
    for step in range(1, nband):
        sends[step - 1].wait_recv()
        origin = lax.rem(band + nband - step, nband)
        block = out_ref.at[origin, mine_half]
        relay = remote(block, block, s_rel.at[step], r_rel.at[step], partner)
        relay.start()
        relays.append(relay)
    for relay in relays:
        relay.wait_recv()
    for copy in sends + relays:
        copy.wait_send()
    swap.wait_send()

    @pl.when(z < nz - 1)
    def _():
        rise.wait_send()

    @pl.when(z > 0)
    def _():
        fall.wait_send()


def gather(owner, block, npool, nband):
    half = pltpu.VMEM((TILES // 2, 2, LANES), jnp.float32)
    dma = pltpu.SemaphoreType.DMA
    vmem = pl.BlockSpec(memory_space=pltpu.VMEM)
    return pl.pallas_call(
        functools.partial(gather_kernel, npool, nband),
        out_shape=jax.ShapeDtypeStruct((nband, TILES, 2, LANES), jnp.float32),
        in_specs=[pl.BlockSpec(memory_space=pltpu.SMEM), vmem],
        out_specs=vmem,
        scratch_shapes=[half] * 7 + [dma] * 6 + [dma((nband,))] * 4,
        compiler_params=pltpu.CompilerParams(collective_id=0, has_side_effects=True),
        name="gather",
    )(owner, block)


def shards(npool, nband, orbitals, kpoints, owner):
    block = orbitals.reshape(2, TILES, LANES).transpose(1, 0, 2)
    sources = gather(owner, block, npool, nband)
    total = compute(
        owner, kpoints, sources.reshape(nband * 2 * TILES, LANES), block.reshape(2 * TILES, LANES), jnp.asarray(dft_weights())
    )
    return total.reshape(TILES, 2, LANES).transpose(1, 0, 2).reshape(1, 1, 2, GRID)


def solution(mesh):
    placed = (P("pool", "band", None, None), P(), P())
    body = functools.partial(shards, mesh.shape["pool"], mesh.shape["band"])
    return jax.shard_map(
        body, mesh=mesh, in_specs=placed, out_specs=P("pool", "band", None, None), check_vma=False
    )
```

time: 123 us -> 37.1 us (0.30); the launches traced: 122 us -> 36.9 us
  waiting for transfers between devices: 50.5 us -> 0 us
  Pallas kernels: 0 us -> 33.3 us
  local copies, waits for them, and re-layouts: 34.8 us -> 2.95 us
  between operations: 14.3 us -> 0.67 us
  blocking collectives: 10 us -> 0 us
  other arithmetic: 8.27 us -> 0 us
  matrix products: 3.56 us -> 0 us
    psum x1 -> x0, waiting for transfers between devices: 50.5 us -> none  [shards(): sources = lax.psum(masked, 'pool')]
    pallas_call x0 -> x2, Pallas kernels: none -> 33.3 us  [the longest x1 22 us: gather(): pl.pallas_call(functools.partial(gather_kernel, npool, nband), out_shape=...]
    reshape x10 -> x2, local copies, waits for them, and re-layouts: 14.5 us -> 1.62 us  [shards(): total.reshape(TILES, 2, LANES).transpose(1, 0, 2).reshape(1, 1, 2, GRID)]
    transpose x6 -> x0, local copies, waits for them, and re-layouts: 12 us -> none  [transform(): work = work.reshape(batch, 2, NG, NG, NG).transpose(0, 1, 3, 4, 2).reshap...]
    all_gather x1 -> x0, blocking collectives: 10 us -> none  [shards(): lax.all_gather(sources, 'band', axis=0, tiled=True)]
    another operation x3 -> x0, local copies, waits for them, and re-layouts: 5.93 us -> none  [the longest x1 3.31 us: contribution(): potential = transform(spectrum, inverse).reshape(count_s, count_r, 2, -1)]
    dot_general x6 -> x0, matrix products: 3.56 us -> none  [transform(): jnp.einsum('ij,pjk->pik', matrix, work, precision=lax.Precision.HIGHEST)]
    integer_pow x2 -> x0, other arithmetic: 1.95 us -> none  [the longest x1 1.26 us: coulomb(): (freq[None, None, :] + dvec[2]) ** 2]
  transfers between devices with their start and end apart: 1 -> 0, of which waited for: 1 -> 0; matrix products, arithmetic and copies ran while one was open for 4% -> 0% of each run, Pallas kernels for 0% -> 0%
where the time goes in v1:
time: 37.1 us; the launch traced here: 36.9 us
  Pallas kernels  33.3 us (90%)
  local copies, waits for them, and re-layouts  2.95 us (8%)
  between operations  0.67 us (2%)
    pallas_call x1, Pallas kernels, gather(): pl.pallas_call(functools.partial(gather_kernel, npool, nband), out_shape=...  22 us
    pallas_call x1, Pallas kernels, compute(): pl.pallas_call(functools.partial(compute_kernel, count), out_shape=jax.Sh...  11.3 us
    reshape x2, local copies, waits for them, and re-layouts, shards(): total.reshape(TILES, 2, LANES).transpose(1, 0, 2).reshape(1, 1, 2, GRID)  1.62 us
    unnamed x3, local copies, waits for them, and re-layouts  1.34 us

profile of v1, /device:TPU:0, one launch (start us, length us, event | category | flops | bytes accessed | tf_op | source)
XLA Modules:
  0.0 36.9 jit_solution(2054594207231341305)
XLA Ops:
  0.7 0.0 copy-start
  0.7 0.7 %copy-done = f32[8,3]{0,1:T(4,128)S(1)} copy-done((f32[8,3]{0,1:T(4,128)S(1)}, f32[8,3]{0,1:T(4,128)}, u32[]{:S(2)}) %copy-start) | copy-done | bytes 120
  1.3 0.7 %copy.7.kp_ref = f32[8,3]{1,0:T(8,128)} copy(f32[8,3]{0,1:T(4,128)S(1)} %copy-done) | data formatting | bytes 192 | tf_op args[1]
  2.0 22.0 %gather.1 = f32[4,108,2,128]{3,2,1,0:T(2,128)} custom-call(s32[1]{0:T(128)S(6)} %copy.11.owner_ref, f32[108,2,128]{2,1,0:T(2,128)} %bitcast.12), custom_call_target="tpu_custom_call" | custom-call | tf_op jit(solution)/shard_map/gather/pallas_call | solution.py:348
  24.0 11.3 %exchange.1 = f32[216,128]{1,0:T(8,128)} custom-call(s32[1]{0:T(128)S(6)} %copy.11.owner_ref, f32[8,3]{1,0:T(8,128)} %copy.7.kp_ref, f32[864,128]{1,0:T(8,128)} %bitcast.10, f32[216,128]{1,0:T(8,128)} %bitcast.13, bf16[2,256,256]{2,1,0:T(8,128)(2,1)} %constant.2.clone.w_ref), custom_call_target="tpu_custom_call" | custom-call | tf_op jit(solution)/shard_map/exchange/pallas_call | solution.py:230
  35.3 0.9 %copy.10 = f32[108,2,128]{2,0,1:T(8,128)S(1)} copy(f32[108,2,128]{2,1,0:T(2,128)} %bitcast.14) | data formatting | bytes 221184 | tf_op jit(solution)/shard_map/reshape | solution.py:365
  36.2 0.7 %reshape.19 = f32[1,1,2,13824]{3,2,1,0:T(2,128)} reshape(f32[2,108,128]{2,1,0:T(8,128)S(1)} %bitcast.11) | data formatting | bytes 221184 | tf_op jit(solution)/shard_map/reshape | solution.py:365
Async XLA Ops:
  0.7 0.7 %copy-start = (f32[8,3]{0,1:T(4,128)S(1)}, f32[8,3]{0,1:T(4,128)}, u32[]{:S(2)}) copy-start(f32[8,3]{0,1:T(4,128)} %param.5) | copy-start | bytes 292

commit v2 on v1

--- a/solution.py
+++ b/solution.py
@@ -104,12 +104,12 @@
     return [min(8 * i, 28) for i in range(5)]
 
 
-def compute_kernel(count, owner_ref, kp_ref, src_ref, own_ref, w_ref, out_ref, sre, sim, dre, dim, acc_re, acc_im, ker):
+def compute_kernel(count, owner_ref, kp_ref, src_ref, own_ref, w_ref, out_ref, dre, dim, flat, ker):
     pool = lax.axis_index("pool")
     source = owner_ref[0]
-    d0 = kp_ref[pool, 0] - kp_ref[source, 0]
-    d1 = kp_ref[pool, 1] - kp_ref[source, 1]
-    d2 = kp_ref[pool, 2] - kp_ref[source, 2]
+    d0 = kp_ref[0, pool] - kp_ref[0, source]
+    d1 = kp_ref[1, pool] - kp_ref[1, source]
+    d2 = kp_ref[2, pool] - kp_ref[2, source]
     lane = lane_iota((NG, LANES))
     gc = ((lane % NG + NG // 2) % NG - NG // 2).astype(jnp.float32)
     row = lax.broadcasted_iota(jnp.int32, (NG, LANES), 0)
@@ -120,41 +120,44 @@
         ker[pl.ds(NG * a, NG), :] = (kernel_scale / GRID) / (plane + (ga + d0) ** 2)
 
     lane8 = lane_iota((8, LANES))
-
-    def windows(ref, base, start, ri):
-        return [ref[pl.ds(base + 6 * start + 2 * s + ri, 8, stride=6), :] for s in range(3)]
-
-    def window(rows, j):
-        s, off = divmod(24 * j, LANES)
-        value = rows[s]
-        if off + NG > LANES:
-            value = jnp.where(lane8 >= off, value, rows[s + 1])
-        return value, off
+    row8 = lax.broadcasted_iota(jnp.int32, (8, LANES), 0)
+    carried = (row8 + 16 + lane8 // NG >= NG) & (lane8 < NG * GROUP)
+
+    def tile(ref, base, start, s, ri):
+        if s < 3:
+            return ref[pl.ds(base + 6 * start + 2 * s + ri, 8, stride=6), :]
+        if start + 8 < 36:
+            return ref[pl.ds(base + 6 * (start + 1) + ri, 8, stride=6), :]
+        last = pltpu.roll(ref[pl.ds(base + 6 * start + ri, 8, stride=6), :], 7, 0)
+        first = ref[pl.ds(base + ri, 8, stride=6), :]
+        return jnp.where(row8 == 7, pltpu.roll(first, 7, 0), last)
 
     def shift(value, amount):
         amount %= LANES
         return pltpu.roll(value, amount, 1) if amount else value
 
-    def spread(sets, j):
-        total = None
-        for n in range(GROUP):
-            value, off = window(sets[n], j)
-            moved = shift(value, NG * n - off)
-            total = moved if total is None else jnp.where(lane8 >= NG * n, moved, total)
-        return jnp.where(lane8 < NG * GROUP, total, 0.0)
-
-    def line(re_ref, im_ref, first, stride, step, swapped):
-        values = []
-        for i in range(NG):
-            at = pl.ds(first + step * i, 8, stride=stride) if stride > 1 else pl.ds(first + step * i, 8)
-            pair = (re_ref[at, :], im_ref[at, :])
-            values.append(pair[::-1] if swapped else pair)
-        for i, pair in enumerate(dft24(values)):
-            at = pl.ds(first + step * i, 8, stride=stride) if stride > 1 else pl.ds(first + step * i, 8)
-            if swapped:
-                pair = pair[::-1]
-            re_ref[at, :] = pair[0]
-            im_ref[at, :] = pair[1]
+    def line(re_ref, im_ref, first, stride, step, swapped, before=False, after=False):
+        def at(i):
+            return pl.ds(first + step * i, 8, stride=stride) if stride > 1 else pl.ds(first + step * i, 8)
+
+        def mixed(values, other):
+            return [
+                tuple(jnp.where(carried, values[(i + other) % NG][c], values[i][c]) for c in range(2)) for i in range(NG)
+            ]
+
+        values = [(re_ref[at(i), :], im_ref[at(i), :]) for i in range(NG)]
+        if before:
+            values = mixed(values, -1)
+        if swapped:
+            values = [pair[::-1] for pair in values]
+        values = dft24(values)
+        if swapped:
+            values = [pair[::-1] for pair in values]
+        if after:
+            values = mixed(values, 1)
+        for i, pair in enumerate(values):
+            re_ref[at(i), :] = pair[0]
+            im_ref[at(i), :] = pair[1]
 
     def product(first, second):
         x = jnp.concatenate([first, second], axis=1)
@@ -164,63 +167,91 @@
         y = dot(high, w_ref[0]) + (dot(low, w_ref[0]) + dot(high, w_ref[1]))
         return y[:, :LANES], y[:, LANES:]
 
+    def convolve(part):
+        at = pl.ds(192 * part, 192)
+        re, im = product(dre[at, :], dim[at, :])
+        value = ker[at, :]
+        im, re = product(im * value, re * value)
+        dre[at, :] = re
+        dim[at, :] = im
+
     for group in range(count // GROUP):
+        bases = [2 * TILES * (group * GROUP + n) for n in range(GROUP)]
         for start in starts():
-            own = [windows(own_ref, 0, start, ri) for ri in range(2)]
-            src = [
-                [windows(src_ref, 2 * TILES * (group * GROUP + n), start, ri) for n in range(GROUP)]
-                for ri in range(2)
-            ]
+            density = []
+            for s in range(4):
+                r_re, r_im = (tile(own_ref, 0, start, s, ri) for ri in range(2))
+                cell = []
+                for n in range(GROUP):
+                    s_re, s_im = (tile(src_ref, bases[n], start, s, ri) for ri in range(2))
+                    cell.append((s_re * r_re + s_im * r_im, s_re * r_im - s_im * r_re))
+                density.append(cell)
             for j in range(16):
-                at = pl.ds(16 * start + j, 8, stride=16)
-                r_re = spread([own[0]] * GROUP, j)
-                r_im = spread([own[1]] * GROUP, j)
-                s_re = spread(src[0], j)
-                s_im = spread(src[1], j)
-                sre[at, :] = s_re
-                sim[at, :] = s_im
-                dre[at, :] = s_re * r_re + s_im * r_im
-                dim[at, :] = s_re * r_im - s_im * r_re
+                s, off = divmod(NG * j, LANES)
+                for ri, ref in enumerate((dre, dim)):
+                    total = None
+                    for n in range(GROUP):
+                        lo = off + NG * n
+                        if lo + NG <= LANES:
+                            value = density[s][n][ri]
+                        elif lo >= LANES:
+                            value = density[s + 1][n][ri]
+                        else:
+                            value = jnp.where(lane8 >= LANES // 2, density[s][n][ri], density[s + 1][n][ri])
+                        if total is None:
+                            total = value
+                        else:
+                            lo, hi = lo % LANES, (lo + NG) % LANES
+                            inside = (lane8 >= lo) & (lane8 < hi) if lo < hi else (lane8 >= lo) | (lane8 < hi)
+                            total = jnp.where(inside, value, total)
+                    ref[pl.ds(16 * start + j, 8, stride=16), :] = shift(total, -off)
         for bg in range(3):
-            line(dre, dim, 8 * bg, 1, NG, False)
+            line(dre, dim, 8 * bg, 1, NG, False, before=bg == 2)
         for ag in range(3):
             line(dre, dim, 8 * NG * ag, NG, 1, False)
-        for part in range(3):
-            at = pl.ds(192 * part, 192)
-            re, im = product(dre[at, :], dim[at, :])
-            value = ker[at, :]
-            im, re = product(im * value, re * value)
-            dre[at, :] = re
-            dim[at, :] = im
+        for ag in range(3):
+            convolve(ag)
         for ag in range(3):
             line(dre, dim, 8 * NG * ag, NG, 1, True)
         for bg in range(3):
-            line(dre, dim, 8 * bg, 1, NG, True)
-        for part in range(9):
-            at = pl.ds(64 * part, 64)
-            s_re, s_im, p_re, p_im = sre[at, :], sim[at, :], dre[at, :], dim[at, :]
-            o_re = s_re * p_re - s_im * p_im
-            o_im = s_re * p_im + s_im * p_re
-            if group:
-                o_re += acc_re[at, :]
-                o_im += acc_im[at, :]
-            acc_re[at, :] = o_re
-            acc_im[at, :] = o_im
-
-    for start in starts():
-        for ri, acc in enumerate((acc_re, acc_im)):
-            rows = [None] * 3
-            for j in range(16):
-                value = acc[pl.ds(16 * start + j, 8, stride=16), :]
-                value = value + shift(value, -2 * NG)
-                value = value + shift(value, -NG)
-                s, off = divmod(24 * j, LANES)
-                moved = shift(value, off)
-                rows[s] = moved if rows[s] is None else jnp.where(lane8 >= off, moved, rows[s])
-                if off + NG > LANES:
-                    rows[s + 1] = moved
+            line(dre, dim, 8 * bg, 1, NG, True, after=bg == 2)
+        for start in starts():
+            moved = {}
+            for j in range(-3, 16):
+                for ri, ref in enumerate((dre, dim)):
+                    if j >= 0:
+                        value = ref[pl.ds(16 * start + j, 8, stride=16), :]
+                    elif start:
+                        value = ref[pl.ds(16 * (start - 1) + 16 + j, 8, stride=16), :]
+                    else:
+                        value = pltpu.roll(ref[pl.ds(16 + j, 8, stride=16), :], 1, 0)
+                        end = ref[pl.ds(16 * 28 + 16 + j, 8, stride=16), :]
+                        value = jnp.where(row8 == 0, pltpu.roll(end, 1, 0), value)
+                    moved[j, ri] = shift(value, NG * j)
             for s in range(3):
-                out_ref[pl.ds(6 * start + 2 * s + ri, 8, stride=6), :] = -mixing * rows[s]
+                first = LANES * s // NG
+                last = (LANES * (s + 1) - 1) // NG
+                out_re = out_im = None
+                for n in range(GROUP):
+                    pot = []
+                    for ri in range(2):
+                        value = moved[first - n, ri]
+                        for w in range(first + 1, last + 1):
+                            value = jnp.where(lane8 >= NG * w - LANES * s, moved[w - n, ri], value)
+                        pot.append(value)
+                    s_re, s_im = (tile(src_ref, bases[n], start, s, ri) for ri in range(2))
+                    t_re = s_re * pot[0] - s_im * pot[1]
+                    t_im = s_re * pot[1] + s_im * pot[0]
+                    out_re = t_re if out_re is None else out_re + t_re
+                    out_im = t_im if out_im is None else out_im + t_im
+                for ri, value in enumerate((out_re, out_im)):
+                    at = pl.ds(6 * start + 2 * s + ri, 8, stride=6)
+                    value = -mixing * value
+                    if group:
+                        value = value + flat[group - 1, at, :]
+                    flat[group, at, :] = value
+    for t in range(TILES):
+        out_ref[:, pl.ds(LANES * t, LANES)] = flat[count // GROUP - 1, pl.ds(2 * t, 2), :]
 
 
 def compute(owner, kpoints, sources, own, weights):
@@ -229,10 +260,15 @@
     smem = pl.BlockSpec(memory_space=pltpu.SMEM)
     return pl.pallas_call(
         functools.partial(compute_kernel, count),
-        out_shape=jax.ShapeDtypeStruct((2 * TILES, LANES), jnp.float32),
+        out_shape=jax.ShapeDtypeStruct((2, GRID), jnp.float32),
         in_specs=[smem, smem, vmem, vmem, vmem],
         out_specs=vmem,
-        scratch_shapes=[pltpu.VMEM((ROWS, LANES), jnp.float32)] * 7,
+        scratch_shapes=[
+            pltpu.VMEM((ROWS, LANES), jnp.float32),
+            pltpu.VMEM((ROWS, LANES), jnp.float32),
+            pltpu.VMEM((count // GROUP, 2 * TILES, LANES), jnp.float32),
+            pltpu.VMEM((ROWS, LANES), jnp.float32),
+        ],
         name="exchange",
     )(owner, kpoints, sources, own, weights)
 
@@ -360,9 +396,9 @@
     block = orbitals.reshape(2, TILES, LANES).transpose(1, 0, 2)
     sources = gather(owner, block, npool, nband)
     total = compute(
-        owner, kpoints, sources.reshape(nband * 2 * TILES, LANES), block.reshape(2 * TILES, LANES), jnp.asarray(dft_weights())
+        owner, kpoints.T, sources.reshape(nband * 2 * TILES, LANES), block.reshape(2 * TILES, LANES), jnp.asarray(dft_weights())
     )
-    return total.reshape(TILES, 2, LANES).transpose(1, 0, 2).reshape(1, 1, 2, GRID)
+    return total.reshape(1, 1, 2, GRID)
 
 
 def solution(mesh):

time: 37.1 us -> 26.7 us (0.72)
  Pallas kernels: 33.3 us -> 25.8 us
  local copies, waits for them, and re-layouts: 2.95 us -> 0 us
    pallas_call x1, Pallas kernels: 11.3 us -> 3.8 us  [compute(): pl.pallas_call(functools.partial(compute_kernel, count), out_shape=jax.Sh...]
    reshape x2 -> x0, local copies, waits for them, and re-layouts: 1.62 us -> none  [shards(): total.reshape(TILES, 2, LANES).transpose(1, 0, 2).reshape(1, 1, 2, GRID)]
    unnamed x3 -> x0, local copies, waits for them, and re-layouts: 1.34 us -> none
where the time goes in v2:
time: 26.7 us; the launch traced here: 26.5 us
  Pallas kernels  25.8 us (97%)
  between operations  0.66 us (2%)
    pallas_call x1, Pallas kernels, gather(): pl.pallas_call(functools.partial(gather_kernel, npool, nband), out_shape=...  22 us
    pallas_call x1, Pallas kernels, compute(): pl.pallas_call(functools.partial(compute_kernel, count), out_shape=jax.Sh...  3.8 us

profile of v2, /device:TPU:0, one launch (start us, length us, event | category | flops | bytes accessed | tf_op | source)
XLA Modules:
  0.0 26.5 jit_solution(5764439546522788792)
XLA Ops:
  0.7 22.0 %gather.1 = f32[4,108,2,128]{3,2,1,0:T(2,128)} custom-call(s32[1]{0:T(128)S(6)} %copy.5.owner_ref, f32[108,2,128]{2,1,0:T(2,128)} %bitcast.9), custom_call_target="tpu_custom_call" | custom-call | tf_op jit(solution)/shard_map/gather/pallas_call | solution.py:384
  22.7 3.8 %exchange.1 = f32[2,13824]{1,0:T(2,128)} custom-call(s32[1]{0:T(128)S(6)} %copy.5.owner_ref, f32[3,8]{1,0:T(4,128)} %bitcast.11, f32[864,128]{1,0:T(8,128)} %bitcast.8, f32[216,128]{1,0:T(8,128)} %bitcast.10, bf16[2,256,256]{2,1,0:T(8,128)(2,1)} %constant.2.clone.w_ref), custom_call_target="tpu_custom_call" | custom-call | tf_op jit(solution)/shard_map/exchange/pallas_call | solution.py:261

commit v3 on v2

--- a/solution.py
+++ b/solution.py
@@ -273,12 +273,13 @@
     )(owner, kpoints, sources, own, weights)
 
 
-def gather_kernel(npool, nband, owner_ref, x_ref, out_ref, pair, mine, up, dn, upo, dno, chosen,
+def gather_kernel(npool, nband, pieces, owner_ref, x_ref, out_ref, pair, mine, up, dn, upo, dno,
                   s_pair, r_pair, s_up, r_up, s_dn, r_dn, s_band, r_band, s_rel, r_rel):
     pool, band = lax.axis_index("pool"), lax.axis_index("band")
     nz = npool // 2
     z, core = pool // 2, pool % 2
     half = TILES // 2
+    size = half // pieces
     source = owner_ref[0]
     partner = {"pool": 2 * z + 1 - core}
     above = {"pool": lax.rem(pool + 2, npool)}
@@ -294,99 +295,125 @@
     def remote(src, dst, ss, rs, to):
         return pltpu.make_async_remote_copy(src_ref=src, dst_ref=dst, send_sem=ss, recv_sem=rs, device_id=to, device_id_type=MESH)
 
-    swap = remote(x_ref.at[pl.ds(half * (1 - core), half)], pair, s_pair, r_pair, partner)
-    swap.start()
-    swap.wait_recv()
-    keep = x_ref[pl.ds(half * core, half)]
-    got = pair[...]
-    zero = jnp.zeros_like(got)
-    mine[...] = jnp.where(source == pool, keep, jnp.where(source == 2 * z + 1 - core, got, zero))
-
-    rise = remote(upo, up, s_up, r_up, above)
-    fall = remote(dno, dn, s_dn, r_dn, below)
-
-    def go_up():
-        @pl.when(z > 0)
+    def cut(k):
+        return pl.ds(size * k, size)
+
+    swaps = [
+        remote(x_ref.at[pl.ds(half * (1 - core) + size * k, size)], pair.at[cut(k)], s_pair.at[k], r_pair.at[k], partner)
+        for k in range(pieces)
+    ]
+    rises = [remote(upo.at[cut(k)], up.at[cut(k)], s_up.at[k], r_up.at[k], above) for k in range(pieces)]
+    falls = [remote(dno.at[cut(k)], dn.at[cut(k)], s_dn.at[k], r_dn.at[k], below) for k in range(pieces)]
+    spreads = [[None] * nband for _ in range(pieces)]
+    relays = [[None] * nband for _ in range(pieces)]
+    for k in range(pieces):
+        block_at = pl.ds(half * core + size * k, size)
+        for step in range(nband):
+            block = out_ref.at[lax.rem(band + nband - step, nband), block_at]
+            relays[k][step] = remote(block, block, s_rel.at[k, step], r_rel.at[k, step], partner)
+            if step:
+                block = out_ref.at[band, block_at]
+                spreads[k][step] = remote(
+                    block, block, s_band.at[k, step], r_band.at[k, step], {"band": lax.rem(band + step, nband)}
+                )
+    for swap in swaps:
+        swap.start()
+
+    def take(k):
+        swaps[k].wait_recv()
+        keep = x_ref[pl.ds(half * core + size * k, size)]
+        got = pair[cut(k)]
+        other = jnp.where(source == 2 * z + 1 - core, got, jnp.zeros_like(got))
+        mine[cut(k)] = jnp.where(source == pool, keep, other)
+
+    def finish(k):
+        total = mine[cut(k)]
+        out_ref[band, pl.ds(half * core + size * k, size)] = total + up[cut(k)] + dn[cut(k)]
+        for step in range(1, nband):
+            spreads[k][step].start()
+        relays[k][0].start()
+
+    def run(near, near_out, nears, far, far_out, fars, at_near_end, at_far_end):
+        @pl.when(at_near_end)
         def _():
-            rise.wait_recv()
-
-        @pl.when(z == 0)
+            near[...] = jnp.zeros_like(near)
+            for k in range(pieces):
+                take(k)
+                near_out[cut(k)] = mine[cut(k)]
+                nears[k].start()
+
+        @pl.when(jnp.logical_not(at_near_end))
         def _():
-            up[...] = jnp.zeros_like(up)
-
-        @pl.when(z < nz - 1)
+            for k in range(pieces):
+                take(k)
+            for k in range(pieces):
+                nears[k].wait_recv()
+
+                @pl.when(jnp.logical_not(at_far_end))
+                def _():
+                    near_out[cut(k)] = near[cut(k)] + mine[cut(k)]
+                    nears[k].start()
+
+        @pl.when(at_far_end)
         def _():
-            upo[...] = up[...] + mine[...]
-            rise.start()
-
-    def go_down():
-        @pl.when(z < nz - 1)
-        def _():
-            fall.wait_recv()
-
-        @pl.when(z == nz - 1)
-        def _():
-            dn[...] = jnp.zeros_like(dn)
-
-        @pl.when(z > 0)
-        def _():
-            dno[...] = dn[...] + mine[...]
-            fall.start()
+            far[...] = jnp.zeros_like(far)
+
+        for k in range(pieces):
+            @pl.when(jnp.logical_not(at_far_end))
+            def _():
+                fars[k].wait_recv()
+
+            @pl.when(jnp.logical_not(at_near_end))
+            def _():
+                far_out[cut(k)] = far[cut(k)] + mine[cut(k)]
+                fars[k].start()
+
+            finish(k)
+
+    bottom, top = z == 0, z == nz - 1
 
     @pl.when(z < nz // 2)
     def _():
-        go_up()
-        go_down()
+        run(up, upo, rises, dn, dno, falls, bottom, top)
 
     @pl.when(z >= nz // 2)
     def _():
-        go_down()
-        go_up()
-
-    chosen[...] = mine[...] + up[...] + dn[...]
-    mine_half = pl.ds(half * core, half)
-    here = out_ref.at[band, mine_half]
-    sends = []
-    for step in range(1, nband):
-        other = lax.rem(band + step, nband)
-        copy = remote(chosen, here, s_band.at[step], r_band.at[step], {"band": other})
-        copy.start()
-        sends.append(copy)
-    relays = [remote(chosen, here, s_rel.at[0], r_rel.at[0], partner)]
-    relays[0].start()
-    out_ref[band, mine_half] = chosen[...]
-    for step in range(1, nband):
-        sends[step - 1].wait_recv()
-        origin = lax.rem(band + nband - step, nband)
-        block = out_ref.at[origin, mine_half]
-        relay = remote(block, block, s_rel.at[step], r_rel.at[step], partner)
-        relay.start()
-        relays.append(relay)
-    for relay in relays:
-        relay.wait_recv()
-    for copy in sends + relays:
-        copy.wait_send()
-    swap.wait_send()
-
-    @pl.when(z < nz - 1)
-    def _():
-        rise.wait_send()
-
-    @pl.when(z > 0)
-    def _():
-        fall.wait_send()
-
-
-def gather(owner, block, npool, nband):
+        if nz > 1:
+            run(dn, dno, falls, up, upo, rises, top, bottom)
+
+    for k in range(pieces):
+        for step in range(1, nband):
+            spreads[k][step].wait_recv()
+            relays[k][step].start()
+    for k in range(pieces):
+        for step in range(nband):
+            relays[k][step].wait_recv()
+    for k in range(pieces):
+        swaps[k].wait_send()
+        for step in range(nband):
+            relays[k][step].wait_send()
+            if step:
+                spreads[k][step].wait_send()
+
+        @pl.when(jnp.logical_not(top))
+        def _():
+            rises[k].wait_send()
+
+        @pl.when(jnp.logical_not(bottom))
+        def _():
+            falls[k].wait_send()
+
+
+def gather(owner, block, npool, nband, pieces=3):
     half = pltpu.VMEM((TILES // 2, 2, LANES), jnp.float32)
     dma = pltpu.SemaphoreType.DMA
     vmem = pl.BlockSpec(memory_space=pltpu.VMEM)
     return pl.pallas_call(
-        functools.partial(gather_kernel, npool, nband),
-        out_shape=jax.ShapeDtypeStruct((nband, TILES, 2, LANES), jnp.float32),
+        functools.partial(gather_kernel, npool, nband, pieces),
+        out_shape=pltpu.VMEM((nband, TILES, 2, LANES), jnp.float32),
         in_specs=[pl.BlockSpec(memory_space=pltpu.SMEM), vmem],
         out_specs=vmem,
-        scratch_shapes=[half] * 7 + [dma] * 6 + [dma((nband,))] * 4,
+        scratch_shapes=[half] * 6 + [dma((pieces,))] * 6 + [dma((pieces, nband))] * 4,
         compiler_params=pltpu.CompilerParams(collective_id=0, has_side_effects=True),
         name="gather",
     )(owner, block)
@@ -396,7 +423,7 @@
     block = orbitals.reshape(2, TILES, LANES).transpose(1, 0, 2)
     sources = gather(owner, block, npool, nband)
     total = compute(
-        owner, kpoints.T, sources.reshape(nband * 2 * TILES, LANES), block.reshape(2 * TILES, LANES), jnp.asarray(dft_weights())
+        owner, kpoints.T, pltpu.with_memory_space_constraint(sources.reshape(nband * 2 * TILES, LANES), pltpu.VMEM), block.reshape(2 * TILES, LANES), jnp.asarray(dft_weights())
     )
     return total.reshape(1, 1, 2, GRID)
 

time: 26.7 us -> 24.8 us (0.929)
  Pallas kernels: 25.8 us -> 24 us
    pallas_call x1, Pallas kernels: 22 us -> 20.3 us  [gather(): pl.pallas_call(functools.partial(gather_kernel, npool, nband, pieces), ou...]
where the time goes in v3:
time: 24.8 us; the launch traced here: 24.6 us
  Pallas kernels  24 us (97%)
  between operations  0.66 us (3%)
    pallas_call x1, Pallas kernels, gather(): pl.pallas_call(functools.partial(gather_kernel, npool, nband, pieces), ou...  20.3 us
    pallas_call x1, Pallas kernels, compute(): pl.pallas_call(functools.partial(compute_kernel, count), out_shape=jax.Sh...  3.67 us

profile of v3, /device:TPU:0, one launch (start us, length us, event | category | flops | bytes accessed | tf_op | source)
XLA Modules:
  0.0 24.6 jit_solution(2959370733430502653)
XLA Ops:
  0.7 20.3 %gather.1 = f32[4,108,2,128]{3,2,1,0:T(2,128)S(1)} custom-call(s32[1]{0:T(128)S(6)} %copy.5.owner_ref, f32[108,2,128]{2,1,0:T(2,128)} %bitcast.9), custom_call_target="tpu_custom_call" | custom-call | tf_op jit(solution)/shard_map/gather/pallas_call | solution.py:411
  21.0 3.7 %exchange.1 = f32[2,13824]{1,0:T(2,128)} custom-call(s32[1]{0:T(128)S(6)} %copy.5.owner_ref, f32[3,8]{1,0:T(4,128)} %bitcast.11, f32[864,128]{1,0:T(8,128)S(1)} %bitcast.8, f32[216,128]{1,0:T(8,128)} %bitcast.10, bf16[2,256,256]{2,1,0:T(8,128)(2,1)} %constant.2.clone.w_ref), custom_call_target="tpu_custom_call" | custom-call | tf_op jit(solution)/shard_map/exchange/pallas_call | solution.py:261

commit v4 on v3

--- a/solution.py
+++ b/solution.py
@@ -422,8 +422,13 @@
 def shards(npool, nband, orbitals, kpoints, owner):
     block = orbitals.reshape(2, TILES, LANES).transpose(1, 0, 2)
     sources = gather(owner, block, npool, nband)
+    near = functools.partial(pltpu.with_memory_space_constraint, memory_space=pltpu.VMEM)
     total = compute(
-        owner, kpoints.T, pltpu.with_memory_space_constraint(sources.reshape(nband * 2 * TILES, LANES), pltpu.VMEM), block.reshape(2 * TILES, LANES), jnp.asarray(dft_weights())
+        owner,
+        kpoints.T,
+        near(sources.reshape(nband * 2 * TILES, LANES)),
+        near(block.reshape(2 * TILES, LANES)),
+        near(jnp.asarray(dft_weights())),
     )
     return total.reshape(1, 1, 2, GRID)
 

time: 24.8 us -> 24.6 us (level)
  Pallas kernels: 24 us -> 23.7 us
    pallas_call x1, Pallas kernels: 3.67 us -> 3.38 us  [compute(): pl.pallas_call(functools.partial(compute_kernel, count), out_shape=jax.Sh...]
where the time goes in v4:
time: 24.6 us; the launch traced here: 24.4 us
  Pallas kernels  23.7 us (96%)
  between operations  0.69 us (3%)
    pallas_call x1, Pallas kernels, gather(): pl.pallas_call(functools.partial(gather_kernel, npool, nband, pieces), ou...  20.4 us
    pallas_call x1, Pallas kernels, compute(): pl.pallas_call(functools.partial(compute_kernel, count), out_shape=jax.Sh...  3.38 us

profile of v4, /device:TPU:0, one launch (start us, length us, event | category | flops | bytes accessed | tf_op | source)
XLA Modules:
  0.0 24.4 jit_solution(15142853825306582012)
XLA Ops:
  0.7 0.0 copy-start
  0.7 0.0 copy-start.1
  0.7 20.4 %gather.1 = f32[4,108,2,128]{3,2,1,0:T(2,128)S(1)} custom-call(s32[1]{0:T(128)S(6)} %copy.5.owner_ref, f32[108,2,128]{2,1,0:T(2,128)} %bitcast.9), custom_call_target="tpu_custom_call" | custom-call | tf_op jit(solution)/shard_map/gather/pallas_call | solution.py:411
  21.0 0.0 copy-done
  21.1 0.0 copy-done.1
  21.1 3.4 %exchange.1 = f32[2,13824]{1,0:T(2,128)} custom-call(s32[1]{0:T(128)S(6)} %copy.5.owner_ref, f32[3,8]{1,0:T(4,128)} %bitcast.11, f32[864,128]{1,0:T(8,128)S(1)} %bitcast.8, f32[216,128]{1,0:T(8,128)S(1)} %bitcast.10, bf16[2,256,256]{2,1,0:T(8,128)(2,1)S(1)} %copy-done.1), custom_call_target="tpu_custom_call" | custom-call | tf_op jit(solution)/shard_map/exchange/pallas_call | solution.py:261
Async XLA Ops:
  0.7 20.4 %copy-start = (f32[1,1,2,13824]{3,2,1,0:T(2,128)S(1)}, f32[1,1,2,13824]{3,2,1,0:T(2,128)}, u32[]{:S(2)}) copy-start(f32[1,1,2,13824]{3,2,1,0:T(2,128)} %param.4) | copy-start | bytes 331780
  0.7 20.4 %copy-start.1 = (bf16[2,256,256]{2,1,0:T(8,128)(2,1)S(1)}, bf16[2,256,256]{2,1,0:T(8,128)(2,1)}, u32[]{:S(2)}) copy-start(bf16[2,256,256]{2,1,0:T(8,128)(2,1)} %constant.2.clone.w_ref) | copy-start | bytes 786436
